TPU v7x, 32 devices: a whole 2x2x4 slice. The times are simulated.
32 devices in a mesh: pipe: 4 (over x, core), row: 4 (over z), col: 2 (over y).
Axes of the slice: x: 2, y: 2, z: 4, core: 2. Of those that a mesh axis runs over, the one named last changes fastest.
Arguments:
- handoff: bfloat16 [4, 256, 12288], P('pipe', 'col', 'row'), may hold values from -1200 to 1200
- norm_gain: float32 [4, 12288], P('pipe', 'row'), may hold values from 0.1 to 1.9
- norm_shift: float32 [4, 12288], P('pipe', 'row'), may hold values from -3 to 3
- up_weight: bfloat16 [4, 12288, 24576], P('pipe', 'row', 'col'), may hold values from -0.0546875 to 0.0546875
- up_bias: float32 [4, 24576], P('pipe', 'col'), may hold values from -3 to 3
Outputs:
- hidden: bfloat16 [4, 256, 24576], P('pipe', 'row', 'col')
All inputs are finite; a program needn't handle non-finite values.
Results may differ from a plain program's by a relative error of at most 0.018.
Values may be sent and summed in bfloat16 or wider, within the bound.
A program may use at most 128 MiB of HBM per device.

v0:
```python
import jax
import jax.numpy as jnp
from jax import lax
from jax.sharding import PartitionSpec as P

epsilon = 1e-05


def passed_along(value, axis, steps):
    count = lax.axis_size(axis)
    pairs = [(source, (source + steps) % count) for source in range(count)]
    return lax.ppermute(value, axis, pairs)


def normalize(values, row_total, squares, feature_gain, feature_shift, feature_count):
    center = (row_total / feature_count)[:, None]
    spread_sq = (squares / feature_count)[:, None] - center * center
    inverse = lax.rsqrt(spread_sq + epsilon)
    return ((values - center) * inverse * feature_gain + feature_shift).astype(jnp.bfloat16)


def local(handoff, norm_gain, norm_shift, up_weight, up_bias):
    arrived = passed_along(handoff[0], "pipe", 1)
    feature_gain = norm_gain[0]
    feature_shift = norm_shift[0]
    weight_block = up_weight[0]
    bias_block = up_bias[0]
    feature_count = arrived.shape[1] * lax.axis_size("row")
    values = arrived.astype(jnp.float32)
    row_total, squares = lax.psum(
        (jnp.sum(values, axis=1), jnp.sum(values * values, axis=1)), "row"
    )
    own_normed = normalize(values, row_total, squares, feature_gain, feature_shift, feature_count)
    normed = lax.all_gather(own_normed, "col", axis=0, tiled=True)
    summed = lax.psum_scatter(
        jnp.dot(normed, weight_block, preferred_element_type=jnp.float32).astype(jnp.bfloat16),
        "row",
        scatter_dimension=0,
        tiled=True,
    ).astype(jnp.float32)
    preact = summed + bias_block
    return jax.nn.gelu(preact, approximate=True).astype(jnp.bfloat16)[None]


def solution(mesh):
    in_specs = (
        P("pipe", "col", "row"),
        P("pipe", "row"),
        P("pipe", "row"),
        P("pipe", "row", "col"),
        P("pipe", "col"),
    )
    out_specs = P("pipe", "row", "col")
    return jax.shard_map(local, mesh=mesh, in_specs=in_specs, out_specs=out_specs, check_vma=False)
```

profile of v0, /device:TPU:26, one launch (start us, length us, event | category | flops | bytes accessed | tf_op | source)
XLA Modules:
  0.0 209.9 jit_solution(13344893527006407649)
XLA Ops:
  6.5 0.0 all-gather.2.cloned.1.call-start
  6.5 0.0 collective-permute-start
  6.5 11.6 %collective-permute-done = bf16[128,3072]{1,0:T(8,128)(2,1)S(1)} collective-permute-done((bf16[128,3072]{1,0:T(8,128)(2,1)}, bf16[128,3072]{1,0:T(8,128)(2,1)S(1)}, u32[]{:S(2)}, u32[]{:S(2)}) %collective-permute-start) | collective-permute-done | bytes 786464 | tf_op jit(solution)/shard_map/ppermute | solution.py:12
  18.2 0.3 convert_reduce_fusion
  18.5 8.1 %all-reduce = (f32[128]{0:T(128)S(1)}, f32[128]{0:T(128)S(1)}) all-reduce(f32[128]{0:T(128)S(1)} %get-tuple-element.6, f32[128]{0:T(128)S(1)} %get-tuple-element.5), channel_id=1, replica_groups=mesh['pipe'=4,'row'=4,'col'=2] {'row'}, use_global_device_ids=true, to_apply=%region_3.0 | all-reduce | flops 256 | bytes 2048 | tf_op jit(solution)/shard_map/psum | solution.py:30
  26.6 2.0 fusion.16
  28.6 0.0 all-gather.2.cloned.1.call-update
  28.6 0.0 reduce-scatter.2.cloned.1.call-start
  28.6 29.1 %all-gather.2.cloned.1.call-done = bf16[256,3072]{1,0:T(8,128)(2,1)} async-done(((bf16[128,3072]{1,0:T(8,128)(2,1)}), bf16[256,3072]{1,0:T(8,128)(2,1)}) %all-gather.2.cloned.1.call-update) | async-done | bytes 1572880 | tf_op jit(solution)/shard_map/all_gather | solution.py:34
  57.7 31.2 %fusion.2 = bf16[256,12288]{1,0:T(8,128)(2,1)} fusion(bf16[256,3072]{1,0:T(8,128)(2,1)} %all-gather.2.cloned.1.call-done, bf16[1,3072,12288]{2,1,0:T(8,128)(2,1)} %param.8), kind=kOutput, calls=%fused_computation.2 | convolution fusion | flops 19330498560 | bytes 83361792 | tf_op jit(solution)/shard_map/dot_general | solution.py:36
  88.9 0.0 copy-start
  88.9 0.0 reduce-scatter.2.cloned.1.call-update
  88.9 110.4 %reduce-scatter.2.cloned.1.call-done = bf16[64,12288]{1,0:T(8,128)(2,1)} async-done(((bf16[256,12288]{1,0:T(8,128)(2,1)}), bf16[64,12288]{1,0:T(8,128)(2,1)}) %reduce-scatter.2.cloned.1.call-update) | async-done | bytes 1572880 | tf_op jit(solution)/shard_map/reduce_scatter | solution.py:35
  199.3 0.0 copy-done
  199.3 3.7 %fusion.18 = bf16[1,64,12288]{2,1,0:T(8,128)(2,1)} fusion(bf16[64,12288]{1,0:T(8,128)(2,1)} %reduce-scatter.2.cloned.1.call-done, f32[12288]{0:T(1024)S(1)} %bitcast.12), kind=kLoop, calls=%fused_computation.20 | loop fusion | flops 8650752 | bytes 3194880 | tf_op jit(solution)/shard_map/broadcast_in_dim | solution.py:42
  (1 shorter events, 0.0 us)
Async XLA Ops:
  6.5 51.2 %all-gather.2.cloned.1.call-start = ((), (), s32[]{:S(2)}) async-start(), calls=%async_computation.1 | async-start | bytes 2359296 | tf_op jit(solution)/shard_map/all_gather | solution.py:34
  6.5 11.6 %collective-permute-start = (bf16[128,3072]{1,0:T(8,128)(2,1)}, bf16[128,3072]{1,0:T(8,128)(2,1)S(1)}, u32[]{:S(2)}, u32[]{:S(2)}) collective-permute-start(bf16[128,3072]{1,0:T(8,128)(2,1)} %bitcast.15), channel_id=1, source_target_pairs={{0,8},{8,16},{16,24},{24,0},{1,9},{9,17},{17,25},{25,1},{2,10},{10... | collective-permute-start | bytes 2359304 | tf_op jit(solution)/shard_map/ppermute | solution.py:12
  28.6 170.7 %reduce-scatter.2.cloned.1.call-start = ((), (), s32[]{:S(2)}) async-start(), calls=%async_computation.2 | async-start | bytes 7864320 | tf_op jit(solution)/shard_map/reduce_scatter | solution.py:35
  88.9 110.5 %copy-start = (f32[1,12288]{1,0:T(1,128)S(1)}, f32[1,12288]{1,0:T(1,128)}, u32[]{:S(2)}) copy-start(f32[1,12288]{1,0:T(1,128)} %param.9) | copy-start | bytes 147460
Sparse Core Ops, SparseCore 0:
  28.7 28.9 all-gather.1
  89.0 110.2 reduce-scatter.1
where the time goes:
time: 212 us; the launch traced here: 210 us
  waiting for transfers between devices  151 us (71%)
  matrix products  31.2 us (15%)
  between operations  13.4 us (6%)
  blocking collectives  8.11 us (4%)
  other arithmetic  6.01 us (3%)
    reduce_scatter x1, waiting for transfers between devices, local(): lax.psum_scatter(jnp.dot(normed, weight_block, preferred_element_type=jnp...  110 us
    dot_general x1, matrix products, local(): jnp.dot(normed, weight_block, preferred_element_type=jnp.float32)  31.2 us
    all_gather x1, waiting for transfers between devices, local(): normed = lax.all_gather(own_normed, 'col', axis=0, tiled=True)  29.1 us
    ppermute x1, waiting for transfers between devices, passed_along(): return lax.ppermute(value, axis, pairs)  11.6 us
    psum x1, blocking collectives, local(): lax.psum((jnp.sum(values, axis=1), jnp.sum(values * values, axis=1)), 'row')  8.11 us
  transfers between devices with their start and end apart: 3, of which 3 were waited for; matrix products, arithmetic and copies ran while one was open for 0% of the time, Pallas kernels for 0%

commit v1 on v0

v1 whole, which is shorter than its diff:
```python
import functools

import jax
import jax.numpy as jnp
from jax import lax
from jax.experimental import pallas as pl
from jax.experimental.pallas import tpu as pltpu
from jax.sharding import PartitionSpec as P

epsilon = 1e-05
MESH = pl.DeviceIdType.MESH
CHUNK = 1024
SUB = 512
SLOTS = 3


def section_kernel(
    stages, rows, cols,
    own_ref, gain_ref, shift_ref, weight_ref, bias_ref, out_ref,
    landed, stats_out, stats_in, normed, weights, partial, received,
    weight_sem, own_send, own_recv, stat_send, stat_recv, part_send, part_recv,
):
    pipe, me, col = lax.axis_index("pipe"), lax.axis_index("row"), lax.axis_index("col")
    after = lax.rem(pipe + 1, stages)
    before = lax.rem(pipe + stages - 1, stages)
    tokens, depth = own_ref.shape
    chunks, _, width = partial.shape
    per_group = rows // cols
    block = tokens // per_group
    feature_count = depth * rows
    steps = cols * chunks
    last = rows - 1

    def weight_copy(step):
        chunk, slot = lax.rem(step, chunks), lax.rem(step, SLOTS)
        columns = pl.ds(pl.multiple_of(chunk * width, width), width)
        return pltpu.make_async_copy(weight_ref.at[:, columns], weights.at[slot], weight_sem.at[slot])

    for step in range(min(SLOTS, steps)):
        weight_copy(step).start()

    barrier = pltpu.get_barrier_semaphore()

    def greet(i, carry):
        pl.semaphore_signal(
            barrier, inc=1, device_id=(before, i // cols, lax.rem(i, cols)), device_id_type=MESH
        )
        return carry

    lax.fori_loop(0, rows * cols, greet, 0)

    @pl.when(me > 0)
    def _():
        pl.semaphore_signal(barrier, inc=1, device_id=(pipe, me - 1, col), device_id_type=MESH)

    @pl.when(me < last)
    def _():
        pl.semaphore_signal(barrier, inc=1, device_id=(pipe, me + 1, col), device_id_type=MESH)

    values = own_ref[...].astype(jnp.float32)
    total = jnp.sum(values, axis=1, keepdims=True)
    squares = jnp.sum(values * values, axis=1, keepdims=True)
    lane = lax.broadcasted_iota(jnp.int32, (tokens, 128), 1)
    both = jnp.where(lane == 0, total, jnp.where(lane == 1, squares, 0.0))
    if tokens < 128:
        both = jnp.concatenate([both, jnp.zeros((128 - tokens, 128), jnp.float32)], axis=0)
    stats_out[...] = both.T[:8]

    neighbours = (me > 0).astype(jnp.int32) + (me < last).astype(jnp.int32)
    pl.semaphore_wait(barrier, rows * cols + neighbours)

    def own_copy(i):
        return pltpu.make_async_remote_copy(
            src_ref=own_ref, dst_ref=landed.at[col], send_sem=own_send.at[i], recv_sem=own_recv.at[col],
            device_id=(after, me, i), device_id_type=MESH,
        )

    def stat_copy(i):
        return pltpu.make_async_remote_copy(
            src_ref=stats_out, dst_ref=stats_in.at[col, me], send_sem=stat_send.at[i],
            recv_sem=stat_recv.at[col, me],
            device_id=(after, i // cols, lax.rem(i, cols)), device_id_type=MESH,
        )

    def start_stat(i, carry):
        stat_copy(i).start()
        return carry

    def start_own(i, carry):
        own_copy(lax.rem(col + i, cols)).start()
        return carry

    lax.fori_loop(0, rows * cols, start_stat, 0)
    lax.fori_loop(0, cols, start_own, 0)

    def to_normed(group):
        def wait_stat(z, carry):
            pltpu.make_async_remote_copy(
                src_ref=stats_out, dst_ref=stats_in.at[group, z], send_sem=stat_send.at[0],
                recv_sem=stat_recv.at[group, z], device_id=(after, me, col), device_id_type=MESH,
            ).wait_recv()
            return carry + stats_in[group, z]

        sums = lax.fori_loop(0, rows, wait_stat, jnp.zeros((8, 128), jnp.float32))
        by_token = jnp.concatenate([sums, jnp.zeros((120, 128), jnp.float32)], axis=0).T[:tokens]
        center = by_token[:, 0:1] / feature_count
        inverse = lax.rsqrt(by_token[:, 1:2] / feature_count - center * center + epsilon)
        pltpu.make_async_remote_copy(
            src_ref=own_ref, dst_ref=landed.at[group], send_sem=own_send.at[0],
            recv_sem=own_recv.at[group], device_id=(after, me, col), device_id_type=MESH,
        ).wait_recv()
        piece = 256
        for lower in range(0, depth, piece):
            part = landed[group, :, lower:lower + piece].astype(jnp.float32)
            scaled = (part - center) * inverse * gain_ref[:, lower:lower + piece]
            normed[:, lower:lower + piece] = (scaled + shift_ref[:, lower:lower + piece]).astype(jnp.bfloat16)

    def rows_of(b):
        return pl.ds(pl.multiple_of(b * block, block), block)

    def send(chunk, b, target, place):
        return pltpu.make_async_remote_copy(
            src_ref=partial.at[chunk, rows_of(b)], dst_ref=received.at[chunk, place],
            send_sem=part_send.at[chunk, b], recv_sem=part_recv.at[chunk, place],
            device_id=(pipe, target, col), device_id_type=MESH,
        )

    def arrival(chunk, b, place):
        send(chunk, b, me, place).wait_recv()
        return received[chunk, place].astype(jnp.float32)

    def group_of(phase):
        return lax.rem(col + phase, cols)

    def forward(chunk, b):
        @pl.when((b > me) & (me > 0))
        def _():
            own = partial[chunk, rows_of(b)].astype(jnp.float32)
            partial[chunk, rows_of(b)] = (own + arrival(chunk, b, b + 1)).astype(jnp.bfloat16)
            send(chunk, b, me + 1, b + 1).start()

        @pl.when((b < me) & (me < last))
        def _():
            own = partial[chunk, rows_of(b)].astype(jnp.float32)
            partial[chunk, rows_of(b)] = (own + arrival(chunk, b, b)).astype(jnp.bfloat16)
            send(chunk, b, me - 1, b).start()

        @pl.when(b == me)
        def _():
            @pl.when(me > 0)
            def _():
                send(chunk, b, me, b + 1).wait_recv()

            @pl.when(me < last)
            def _():
                send(chunk, b, me, b).wait_recv()

            columns = pl.ds(pl.multiple_of(chunk * width, width), width)
            preact = partial[chunk, rows_of(b)].astype(jnp.float32) + bias_ref[:, columns]
            left = jnp.where(me > 0, received[chunk, b + 1].astype(jnp.float32), 0.0)
            right = jnp.where(me < last, received[chunk, b].astype(jnp.float32), 0.0)
            preact = preact + left + right
            out_ref[:, columns] = jax.nn.gelu(preact, approximate=True).astype(jnp.bfloat16)

    def relay(index, carry):
        chunk, group = lax.rem(index, chunks), group_of(index // chunks)
        for i in range(per_group):
            forward(chunk, group * per_group + i)
        return carry

    inner = (me > 0) & (me < last)

    def phase_body(phase, carry):
        group = group_of(phase)
        to_normed(group)

        def chunk_body(chunk, carry):
            step = phase * chunks + chunk
            slot = lax.rem(step, SLOTS)
            weight_copy(step).wait()
            lines = pl.ds(pl.multiple_of(group * tokens, tokens), tokens)
            for lower in range(0, width, SUB):
                product = jnp.dot(
                    normed[...], weights[slot, :, lower:lower + SUB], preferred_element_type=jnp.float32
                )
                partial[chunk, lines, lower:lower + SUB] = product.astype(jnp.bfloat16)

            @pl.when(step + SLOTS < steps)
            def _():
                weight_copy(step + SLOTS).start()

            for i in range(per_group):
                b = group * per_group + per_group - 1 - i

                @pl.when((me == 0) & (b > 0))
                def _():
                    send(chunk, b, me + 1, b + 1).start()

            for i in range(per_group):
                b = group * per_group + i

                @pl.when((me == last) & (b < last))
                def _():
                    send(chunk, b, me - 1, b).start()

            late = step - chunks

            @pl.when(inner & (late >= 0) & (lax.rem(late + chunks, 2) == 0))
            def _():
                relay(late // 2, 0)

            return carry

        return lax.fori_loop(0, chunks, chunk_body, carry)

    lax.fori_loop(0, cols, phase_body, 0)
    done = len([late for late in range(steps - chunks) if (late + chunks) % 2 == 0])
    lax.fori_loop(jnp.where(inner, done, 0), steps, relay, 0)

    def finish(i, carry):
        chunk, b = i // rows, lax.rem(i, rows)

        @pl.when(b != me)
        def _():
            send(chunk, b, me, b).wait_send()

        return carry

    lax.fori_loop(0, chunks * rows, finish, 0)

    def finish_stat(i, carry):
        stat_copy(i).wait_send()
        return carry

    def finish_own(i, carry):
        own_copy(i).wait_send()
        return carry

    lax.fori_loop(0, rows * cols, finish_stat, 0)
    lax.fori_loop(0, cols, finish_own, 0)


def local(stages, rows, cols, handoff, norm_gain, norm_shift, up_weight, up_bias):
    own = handoff[0]
    tokens, depth = own.shape
    hidden = up_weight.shape[2]
    width = min(CHUNK, hidden)
    chunks = hidden // width
    micro = tokens * cols
    block = micro // rows
    vmem = pl.BlockSpec(memory_space=pltpu.VMEM)
    result = pl.pallas_call(
        functools.partial(section_kernel, stages, rows, cols),
        out_shape=jax.ShapeDtypeStruct((block, hidden), jnp.bfloat16),
        in_specs=[vmem, vmem, vmem, pl.BlockSpec(memory_space=pl.ANY), vmem],
        out_specs=vmem,
        scratch_shapes=[
            pltpu.VMEM((cols, tokens, depth), jnp.bfloat16),
            pltpu.VMEM((8, 128), jnp.float32),
            pltpu.VMEM((cols, rows, 8, 128), jnp.float32),
            pltpu.VMEM((tokens, depth), jnp.bfloat16),
            pltpu.VMEM((SLOTS, depth, width), jnp.bfloat16),
            pltpu.VMEM((chunks, micro, width), jnp.bfloat16),
            pltpu.VMEM((chunks, rows + 1, block, width), jnp.bfloat16),
            pltpu.SemaphoreType.DMA((SLOTS,)),
            pltpu.SemaphoreType.DMA((cols,)),
            pltpu.SemaphoreType.DMA((cols,)),
            pltpu.SemaphoreType.DMA((rows * cols,)),
            pltpu.SemaphoreType.DMA((cols, rows)),
            pltpu.SemaphoreType.DMA((chunks, rows)),
            pltpu.SemaphoreType.DMA((chunks, rows + 1)),
        ],
        compiler_params=pltpu.CompilerParams(
            collective_id=0, has_side_effects=True, vmem_limit_bytes=60 * 1024 * 1024
        ),
    )(own, norm_gain, norm_shift, up_weight[0], up_bias)
    return result[None]


def solution(mesh):
    in_specs = (
        P("pipe", "col", "row"),
        P("pipe", "row"),
        P("pipe", "row"),
        P("pipe", "row", "col"),
        P("pipe", "col"),
    )
    out_specs = P("pipe", "row", "col")
    sizes = mesh.shape["pipe"], mesh.shape["row"], mesh.shape["col"]
    return jax.shard_map(
        functools.partial(local, *sizes), mesh=mesh, in_specs=in_specs, out_specs=out_specs, check_vma=False
    )
```

time: 212 us -> 173 us (0.82)
  Pallas kernels: 0 us -> 170 us
  waiting for transfers between devices: 151 us -> 0 us
  matrix products: 31.2 us -> 0 us
  between operations: 13.4 us -> 0.01 us
  blocking collectives: 8.11 us -> 0 us
  other arithmetic: 6.01 us -> 0 us
  local copies, waits for them, and re-layouts: 0.01 us -> 2.65 us
    pallas_call x0 -> x1, Pallas kernels: none -> 170 us  [local(): pl.pallas_call(functools.partial(section_kernel, stages, rows, cols), out...]
    reduce_scatter x1 -> x0, waiting for transfers between devices: 110 us -> none  [local(): lax.psum_scatter(jnp.dot(normed, weight_block, preferred_element_type=jnp...]
    dot_general x1 -> x0, matrix products: 31.2 us -> none  [local(): jnp.dot(normed, weight_block, preferred_element_type=jnp.float32)]
    all_gather x1 -> x0, waiting for transfers between devices: 29.1 us -> none  [local(): normed = lax.all_gather(own_normed, 'col', axis=0, tiled=True)]
    ppermute x1 -> x0, waiting for transfers between devices: 11.6 us -> none  [passed_along(): return lax.ppermute(value, axis, pairs)]
    psum x1 -> x0, blocking collectives: 8.11 us -> none  [local(): lax.psum((jnp.sum(values, axis=1), jnp.sum(values * values, axis=1)), 'row')]
    broadcast_in_dim x1 -> x0, other arithmetic: 3.72 us -> none  [local(): return jax.nn.gelu(preact, approximate=True).astype(jnp.bfloat16)[None]]
    unnamed x2 -> x1, local copies, waits for them, and re-layouts: 0.01 us -> 2.65 us
  transfers between devices with their start and end apart: 3 -> 0, of which waited for: 3 -> 0; matrix products, arithmetic and copies ran while one was open for 0% -> 0% of each run, Pallas kernels for 0% -> 0%
where the time goes in v1:
time: 173 us
  Pallas kernels  170 us (98%)
  local copies, waits for them, and re-layouts  2.65 us (2%)
    pallas_call x1, Pallas kernels, local(): pl.pallas_call(functools.partial(section_kernel, stages, rows, cols), out...  170 us

profile of v1, /device:TPU:26, one launch (start us, length us, event | category | flops | bytes accessed | tf_op | source)
XLA Modules:
  0.0 172.6 jit_solution(11987868190319554019)
XLA Ops:
  0.0 170.0 %shard_map.55 = bf16[64,12288]{1,0:T(8,128)(2,1)} custom-call(bf16[128,3072]{1,0:T(8,128)(2,1)} %bitcast.4, f32[1,3072]{1,0:T(1,128)} %gain_ref.1, f32[1,3072]{1,0:T(1,128)} %shift_ref.1, bf16[3072,12288]{1,0:T(8,128)(2,1)} %bitcast.1.weight_ref, f32[1,12288]{1,0:T(1,128)} %bias_ref.1), custom_call_target="tpu_custom_call" | custom-call | tf_op jit(solution)/shard_map/pallas_call | solution.py:252
  170.0 2.7 %copy.7 = bf16[1,64,12288]{2,1,0:T(8,128)(2,1)} copy(bf16[1,64,12288]{2,1,0:T(8,128)(2,1)} %bitcast.3) | data formatting | bytes 3145728

commit v2 on v1

--- a/solution.py
+++ b/solution.py
@@ -12,6 +12,7 @@
 CHUNK = 1024
 SUB = 512
 SLOTS = 3
+LAG = 2
 
 
 def section_kernel(
@@ -132,7 +133,7 @@
     def group_of(phase):
         return lax.rem(col + phase, cols)
 
-    def forward(chunk, b):
+    def pass_on(chunk, b):
         @pl.when((b > me) & (me > 0))
         def _():
             own = partial[chunk, rows_of(b)].astype(jnp.float32)
@@ -145,6 +146,7 @@
             partial[chunk, rows_of(b)] = (own + arrival(chunk, b, b)).astype(jnp.bfloat16)
             send(chunk, b, me - 1, b).start()
 
+    def conclude(chunk, b):
         @pl.when(b == me)
         def _():
             @pl.when(me > 0)
@@ -165,7 +167,40 @@
     def relay(index, carry):
         chunk, group = lax.rem(index, chunks), group_of(index // chunks)
         for i in range(per_group):
-            forward(chunk, group * per_group + i)
+            pass_on(chunk, group * per_group + i)
+        return carry
+
+    def final(index, carry):
+        chunk, group = lax.rem(index, chunks), group_of(index // chunks)
+        for i in range(per_group):
+            conclude(chunk, group * per_group + i)
+        return carry
+
+    half = chunks // 2
+    paced = cols == 2 and rows == 4 and chunks % 2 == 0
+    first_leads = lax.rem(me + col, 2) == 0
+
+    def pace(turn, carry):
+        one = turn - jnp.where(first_leads, 0, LAG)
+        two = turn - half - jnp.where(first_leads, LAG, 0)
+
+        @pl.when((one >= 0) & (one < chunks))
+        def _():
+            relay(one, 0)
+
+        @pl.when((two >= 0) & (two < chunks))
+        def _():
+            relay(chunks + two, 0)
+
+        for i in range(2):
+            @pl.when((turn >= chunks) & (turn < chunks + half))
+            def _():
+                final(2 * (turn - chunks) + i, 0)
+
+            @pl.when(turn >= chunks + LAG)
+            def _():
+                final(chunks + 2 * (turn - chunks - LAG) + i, 0)
+
         return carry
 
     inner = (me > 0) & (me < last)
@@ -207,7 +242,7 @@
 
             @pl.when(inner & (late >= 0) & (lax.rem(late + chunks, 2) == 0))
             def _():
-                relay(late // 2, 0)
+                pace(late // 2, 0) if paced else relay(late // 2, 0)
 
             return carry
 
@@ -215,7 +250,18 @@
 
     lax.fori_loop(0, cols, phase_body, 0)
     done = len([late for late in range(steps - chunks) if (late + chunks) % 2 == 0])
-    lax.fori_loop(jnp.where(inner, done, 0), steps, relay, 0)
+
+    @pl.when(inner)
+    def _():
+        if paced:
+            lax.fori_loop(half, chunks + half + LAG, pace, 0)
+        else:
+            lax.fori_loop(done, steps, relay, 0)
+            lax.fori_loop(0, steps, final, 0)
+
+    @pl.when(jnp.logical_not(inner))
+    def _():
+        lax.fori_loop(0, steps, final, 0)
 
     def finish(i, carry):
         chunk, b = i // rows, lax.rem(i, rows)

time: 173 us -> 138 us (0.80)
  Pallas kernels: 170 us -> 133 us
    pallas_call x1, Pallas kernels: 170 us -> 133 us  [local(): pl.pallas_call(functools.partial(section_kernel, stages, rows, cols), out...]
where the time goes in v2:
time: 138 us; the launch traced here: 136 us
  Pallas kernels  133 us (96%)
  local copies, waits for them, and re-layouts  2.65 us (2%)
    pallas_call x1, Pallas kernels, local(): pl.pallas_call(functools.partial(section_kernel, stages, rows, cols), out...  133 us

profile of v2, /device:TPU:26, one launch (start us, length us, event | category | flops | bytes accessed | tf_op | source)
XLA Modules:
  0.0 136.0 jit_solution(14471402733875209237)
XLA Ops:
  0.0 133.3 %shard_map.55 = bf16[64,12288]{1,0:T(8,128)(2,1)} custom-call(bf16[128,3072]{1,0:T(8,128)(2,1)} %bitcast.4, f32[1,3072]{1,0:T(1,128)} %gain_ref.1, f32[1,3072]{1,0:T(1,128)} %shift_ref.1, bf16[3072,12288]{1,0:T(8,128)(2,1)} %bitcast.1.weight_ref, f32[1,12288]{1,0:T(1,128)} %bias_ref.1), custom_call_target="tpu_custom_call" | custom-call | tf_op jit(solution)/shard_map/pallas_call | solution.py:298
  133.3 2.7 %copy.7 = bf16[1,64,12288]{2,1,0:T(8,128)(2,1)} copy(bf16[1,64,12288]{2,1,0:T(8,128)(2,1)} %bitcast.3) | data formatting | bytes 3145728
